TPU v7x, 128 devices: a whole 4x4x4 slice. The times are simulated.
128 devices in a mesh: head: 16 (over y_lo, z, core), blk: 8 (over x, y_hi).
Axes of the slice: x: 4, y: 4 (y_hi: 2, y_lo: 2; y = y_hi * 2 + y_lo), z: 4, core: 2. Of those that a mesh axis runs over, the one named last changes fastest.
Arguments:
- query_head_matrix: bfloat16 [16384, 8192], P(('blk', 'head')), may hold values from -8 to 8
- key_matrix: bfloat16 [16384, 1024], P(('blk', 'head')), may hold values from -8 to 8
- value_matrix: bfloat16 [16384, 1024], P(('blk', 'head')), may hold values from -6 to 6
- output_gradient: bfloat16 [16384, 8192], P(('blk', 'head')), may hold values from -6 to 6
- span_lengths: int32 [62], replicated, may hold values from 1 to 512, 15872 in all
Outputs:
- attended: bfloat16 [16384, 8192], P(('blk', 'head'))
- query_grad: bfloat16 [16384, 8192], P(('blk', 'head'))
- key_gradient: bfloat16 [16384, 1024], P(('blk', 'head'))
- value_gradient: bfloat16 [16384, 1024], P(('blk', 'head'))
Inputs may be any that keep to these rules, and one draw needn't show every extreme that they name: `span_lengths`: the 62 span lengths sum to 15872, and the longest span holds exactly 512 tokens.
All inputs are finite; a program needn't handle non-finite values.
Results may differ from a plain program's by a relative error of at most 0.02.
Values may be sent and summed in bfloat16 or wider, within the bound.
No kernel may reach another device: no remote copies, remote signals or barrier semaphores. Data moves between devices by JAX's collectives and lax.ppermute only.
A program may use at most 128 MiB of HBM per device.

v0:
```python
import math
import jax
import jax.numpy as jnp
from jax import lax
from jax.sharding import PartitionSpec as P

QUERY_HEADS = 64
KEY_VALUE_HEADS = 8
HEAD_WIDTH = 128
QLEN = 512
MOST = 512
masked_score = -1e30


def passed_along(block, axis, distance):
    devices = range(lax.axis_size(axis))
    route = [(i - distance, i) for i in devices if i - distance in devices]
    return lax.ppermute(block, axis, route)


def broadcast(block, axis, holder):
    block = jnp.where(lax.axis_index(axis) == holder, block, jnp.zeros_like(block))
    return lax.psum(block, axis)


def merged_2(part, axis, combine):
    gathered = jax.tree.map(lambda a: lax.all_gather(a, axis), part)

    def take(source):
        return jax.tree.map(lambda a: lax.dynamic_index_in_dim(a, source, 0, False), gathered)

    return lax.fori_loop(
        1, lax.axis_size(axis), lambda source, state: combine(state, take(source)), take(0)
    )


def segment_of(span_lengths, positions, context):
    starts = jnp.cumsum(span_lengths) - span_lengths
    found_index = jnp.sum((starts[None, :] <= positions[:, None]).astype(jnp.int32), axis=1) - 1
    return jnp.where(positions >= context, span_lengths.shape[0], found_index)


def combine_parts(left_part, right_part):
    left_max, left_sum, left_acc = left_part
    right_max, right_sum, right_acc = right_part
    joint_max = jnp.maximum(left_max, right_max)
    left_factor = jnp.exp(left_max - joint_max)
    right_factor = jnp.exp(right_max - joint_max)
    joint_sum = left_sum * left_factor + right_sum * right_factor
    joint_acc = left_acc * left_factor[..., None] + right_acc * right_factor[..., None]
    return (joint_max, joint_sum, joint_acc)


def shards(query_head_matrix, key_matrix, value_matrix, output_gradient, span_lengths):
    head_total_count = lax.axis_size("head")
    cycle_count = lax.axis_size("blk")
    cycle_index = lax.axis_index("blk")
    local_token_count = query_head_matrix.shape[0]
    shard_rows = local_token_count * head_total_count
    context = shard_rows * cycle_count - QLEN
    local_heads = QUERY_HEADS // head_total_count
    replica_count = head_total_count // KEY_VALUE_HEADS
    tile_rows = min(512, shard_rows)
    tile_total = shard_rows // tile_rows
    score_scale = 1.0 / math.sqrt(HEAD_WIDTH)
    query_matrix = query_head_matrix.reshape(local_token_count, QUERY_HEADS, HEAD_WIDTH)
    output_adjoint = output_gradient.reshape(local_token_count, QUERY_HEADS, HEAD_WIDTH)
    key_head_rows = key_matrix.reshape(local_token_count, KEY_VALUE_HEADS, HEAD_WIDTH)
    value_head_rows = value_matrix.reshape(local_token_count, KEY_VALUE_HEADS, HEAD_WIDTH)
    key_send = jnp.repeat(key_head_rows, replica_count, axis=1)
    value_send = jnp.repeat(value_head_rows, replica_count, axis=1)
    query_head, grad_head, key_recv, value_recv = (
        lax.all_to_all(query_matrix, "head", split_axis=1, concat_axis=0, tiled=True),
        lax.all_to_all(output_adjoint, "head", split_axis=1, concat_axis=0, tiled=True),
        lax.all_to_all(key_send, "head", split_axis=1, concat_axis=0, tiled=True),
        lax.all_to_all(value_send, "head", split_axis=1, concat_axis=0, tiled=True),
    )
    key_local = key_recv.reshape(shard_rows, HEAD_WIDTH)
    value_local = value_recv.reshape(shard_rows, HEAD_WIDTH)
    rim_rows = jnp.stack([key_local[shard_rows - MOST :], value_local[shard_rows - MOST :]])
    rim_rows = passed_along(rim_rows, "blk", 1)
    key_window = jnp.concatenate([rim_rows[0], key_local])
    value_window = jnp.concatenate([rim_rows[1], value_local])
    base_row = cycle_index * shard_rows
    query_pos = base_row + jnp.arange(shard_rows, dtype=jnp.int32)
    window_pos = base_row - MOST + jnp.arange(shard_rows + MOST, dtype=jnp.int32)
    query_seg = segment_of(span_lengths, query_pos, context)
    window_seg = segment_of(span_lengths, window_pos, context)
    key_context = query_pos < context

    def tile_scores(tile_index):
        first_row = tile_index * tile_rows
        window_rows = tile_rows + MOST
        query_tile = lax.dynamic_slice_in_dim(query_head, first_row, tile_rows, 0)
        key_tile = lax.dynamic_slice_in_dim(key_window, first_row, window_rows, 0)
        value_tile = lax.dynamic_slice_in_dim(value_window, first_row, window_rows, 0)
        row_seg = lax.dynamic_slice_in_dim(query_seg, first_row, tile_rows, 0)
        row_pos = lax.dynamic_slice_in_dim(query_pos, first_row, tile_rows, 0)
        key_seg = lax.dynamic_slice_in_dim(window_seg, first_row, window_rows, 0)
        key_pos = lax.dynamic_slice_in_dim(window_pos, first_row, window_rows, 0)
        visible = (row_seg[:, None] == key_seg[None, :]) & (key_pos[None, :] <= row_pos[:, None])
        scores = (
            jnp.einsum("qhd,kd->hqk", query_tile, key_tile, preferred_element_type=jnp.float32)
            * score_scale
        )
        scores = jnp.where(visible[None], scores, masked_score)
        return (first_row, query_tile, key_tile, value_tile, visible, scores)

    def forward_tile(tile_index):
        first_row, query_tile, key_tile, value_tile, visible, scores = tile_scores(tile_index)
        row_max = jnp.max(scores, axis=2)
        weights = jnp.where(visible[None], jnp.exp(scores - row_max[..., None]), 0.0)
        row_total = jnp.sum(weights, axis=2)
        summed = jnp.einsum(
            "hqk,kd->qhd",
            weights.astype(jnp.bfloat16),
            value_tile,
            preferred_element_type=jnp.float32,
        )
        return (row_max.T, row_total.T, summed)

    tile_max, tile_sum, tile_acc = lax.map(forward_tile, jnp.arange(tile_total))
    tile_max = tile_max.reshape(shard_rows, local_heads)
    tile_sum = tile_sum.reshape(shard_rows, local_heads)
    tile_acc = tile_acc.reshape(shard_rows, local_heads, HEAD_WIDTH)
    question_start = shard_rows - QLEN
    last_cycle = cycle_count - 1
    own_rows = jnp.stack([query_head[question_start:], grad_head[question_start:]])
    shared_rows = broadcast(own_rows, "blk", last_cycle)
    question_query = jnp.moveaxis(shared_rows[0], 1, 0)
    question_grad = jnp.moveaxis(shared_rows[1], 1, 0)

    def question_forward(query_one):
        scores = (
            jnp.einsum("qd,kd->qk", query_one, key_local, preferred_element_type=jnp.float32)
            * score_scale
        )
        scores = jnp.where(key_context[None, :], scores, masked_score)
        row_max = jnp.max(scores, axis=1)
        weights = jnp.where(key_context[None, :], jnp.exp(scores - row_max[:, None]), 0.0)
        row_total = jnp.sum(weights, axis=1)
        summed = jnp.dot(
            weights.astype(jnp.bfloat16), value_local, preferred_element_type=jnp.float32
        )
        return (row_max, row_total, summed)

    part_max, part_sum, part_acc = lax.map(question_forward, question_query)
    merged = merged_2((part_max, part_sum, part_acc), "blk", combine_parts)
    holder = cycle_index == last_cycle
    own_stats = (
        tile_max[question_start:].T,
        tile_sum[question_start:].T,
        jnp.moveaxis(tile_acc[question_start:], 1, 0),
    )
    joined = combine_parts(own_stats, merged)
    question_max = jnp.where(holder, joined[0], own_stats[0]).T
    question_sum = jnp.where(holder, joined[1], own_stats[1]).T
    question_acc = jnp.moveaxis(jnp.where(holder, joined[2], own_stats[2]), 0, 1)
    row_max = jnp.concatenate([tile_max[:question_start], question_max])
    row_total = jnp.concatenate([tile_sum[:question_start], question_sum])
    row_acc = jnp.concatenate([tile_acc[:question_start], question_acc])
    attended_head = (row_acc / row_total[..., None]).astype(jnp.bfloat16)
    row_lse = row_max + jnp.log(row_total)
    attended_back = lax.all_to_all(attended_head, "head", split_axis=0, concat_axis=1, tiled=True)
    row_dd = jnp.sum(grad_head.astype(jnp.float32) * attended_head.astype(jnp.float32), axis=2)
    own_stat = jnp.stack([row_lse[question_start:].T, row_dd[question_start:].T])
    shared_stat = broadcast(own_stat, "blk", last_cycle)

    def backward_tile(running, tile_index):
        key_grads, value_grads = running
        first_row, query_tile, key_tile, value_tile, visible, scores = tile_scores(tile_index)
        lse_tile = lax.dynamic_slice_in_dim(row_lse, first_row, tile_rows, 0).T
        dd_tile = lax.dynamic_slice_in_dim(row_dd, first_row, tile_rows, 0).T
        grad_tile = lax.dynamic_slice_in_dim(grad_head, first_row, tile_rows, 0)
        probabilities = jnp.where(visible[None], jnp.exp(scores - lse_tile[..., None]), 0.0)
        value_part = jnp.einsum(
            "hqk,qhd->kd",
            probabilities.astype(jnp.bfloat16),
            grad_tile,
            preferred_element_type=jnp.float32,
        )
        prob_grad = jnp.einsum(
            "qhd,kd->hqk", grad_tile, value_tile, preferred_element_type=jnp.float32
        )
        score_grad = (probabilities * (prob_grad - dd_tile[..., None])).astype(jnp.bfloat16)
        query_part = (
            jnp.einsum("hqk,kd->qhd", score_grad, key_tile, preferred_element_type=jnp.float32)
            * score_scale
        )
        key_part = (
            jnp.einsum("hqk,qhd->kd", score_grad, query_tile, preferred_element_type=jnp.float32)
            * score_scale
        )
        window_rows = tile_rows + MOST
        key_grads = lax.dynamic_update_slice_in_dim(
            key_grads,
            lax.dynamic_slice_in_dim(key_grads, first_row, window_rows, 0) + key_part,
            first_row,
            0,
        )
        value_grads = lax.dynamic_update_slice_in_dim(
            value_grads,
            lax.dynamic_slice_in_dim(value_grads, first_row, window_rows, 0) + value_part,
            first_row,
            0,
        )
        return ((key_grads, value_grads), query_part)

    empty_window = jnp.zeros((shard_rows + MOST, HEAD_WIDTH), jnp.float32)
    (key_grads, value_grads), query_tiles = lax.scan(
        backward_tile, (empty_window, empty_window), jnp.arange(tile_total)
    )
    query_grads = query_tiles.reshape(shard_rows, local_heads, HEAD_WIDTH)

    def question_backward(parts):
        query_one, grad_one, lse_one, dd_one = parts
        scores = (
            jnp.einsum("qd,kd->qk", query_one, key_local, preferred_element_type=jnp.float32)
            * score_scale
        )
        probabilities = jnp.where(key_context[None, :], jnp.exp(scores - lse_one[:, None]), 0.0)
        value_part = jnp.einsum(
            "qk,qd->kd",
            probabilities.astype(jnp.bfloat16),
            grad_one,
            preferred_element_type=jnp.float32,
        )
        prob_grad = jnp.einsum(
            "qd,kd->qk", grad_one, value_local, preferred_element_type=jnp.float32
        )
        score_grad = (probabilities * (prob_grad - dd_one[:, None])).astype(jnp.bfloat16)
        query_part = (
            jnp.dot(score_grad, key_local, preferred_element_type=jnp.float32) * score_scale
        )
        key_part = (
            jnp.einsum("qk,qd->kd", score_grad, query_one, preferred_element_type=jnp.float32)
            * score_scale
        )
        return (query_part, key_part, value_part)

    quest_query_parts, quest_key_parts, quest_value_parts = lax.map(
        question_backward, (question_query, question_grad, shared_stat[0], shared_stat[1])
    )
    question_total = lax.psum(quest_query_parts, "blk")
    question_added = jnp.where(holder, jnp.moveaxis(question_total, 0, 1), 0.0)
    query_grads = jnp.concatenate(
        [query_grads[:question_start], query_grads[question_start:] + question_added]
    )
    dq_head = query_grads.astype(jnp.bfloat16)
    rim_grads = jnp.stack([key_grads[:MOST], value_grads[:MOST]])
    rim_back = passed_along(rim_grads, "blk", -1)
    tail_pad = jnp.zeros((shard_rows - MOST, HEAD_WIDTH), jnp.float32)
    key_total = (
        key_grads[MOST:]
        + jnp.sum(quest_key_parts, axis=0)
        + jnp.concatenate([tail_pad, rim_back[0]])
    )
    value_total = (
        value_grads[MOST:]
        + jnp.sum(quest_value_parts, axis=0)
        + jnp.concatenate([tail_pad, rim_back[1]])
    )
    grads_send = jnp.stack([key_total, value_total], axis=1)
    gradient_received = lax.all_to_all(grads_send, "head", split_axis=0, concat_axis=1, tiled=True)
    gradient_received = jnp.sum(
        gradient_received.reshape(local_token_count, KEY_VALUE_HEADS, replica_count, 2, HEAD_WIDTH),
        axis=2,
    )
    gradient_results = gradient_received.astype(jnp.bfloat16)
    key_gradient = gradient_results[:, :, 0].reshape(
        local_token_count, KEY_VALUE_HEADS * HEAD_WIDTH
    )
    value_gradient = gradient_results[:, :, 1].reshape(
        local_token_count, KEY_VALUE_HEADS * HEAD_WIDTH
    )
    query_back = lax.all_to_all(dq_head, "head", split_axis=0, concat_axis=1, tiled=True)
    attended = attended_back.reshape(local_token_count, QUERY_HEADS * HEAD_WIDTH)
    query_grad = query_back.reshape(local_token_count, QUERY_HEADS * HEAD_WIDTH)
    return (attended, query_grad, key_gradient, value_gradient)


def solution(mesh):
    in_specs = (
        P(("blk", "head"), None),
        P(("blk", "head"), None),
        P(("blk", "head"), None),
        P(("blk", "head"), None),
        P(),
    )
    out_specs = (
        P(("blk", "head"), None),
        P(("blk", "head"), None),
        P(("blk", "head"), None),
        P(("blk", "head"), None),
    )
    return jax.shard_map(shards, mesh=mesh, in_specs=in_specs, out_specs=out_specs, check_vma=False)
```

profile of v0, /device:TPU:1, one launch (start us, length us, event | category | flops | bytes accessed | tf_op | source)
XLA Modules:
  0.0 694.6 jit_solution(15561135243278335553)
XLA Ops:
  7.2 4.1 copy.130
  11.3 7.8 %all-to-all-start.2 = ((bf16[128,64,128]{0,2,1:T(8,128)(2,1)}), bf16[128,64,128]{0,2,1:T(8,128)(2,1)S(1)}, u32[]{:S(2)}, u32[]{:S(2)}) async-start(bf16[128,64,128]{0,2,1:T(8,128)(2,1)} %bitcast.404), calls=%async_computation.2 | async-start | bytes 4194304 | tf_op jit(solution)/shard_map/all_to_all | solution.py:73
  19.1 4.1 copy.137
  23.2 23.5 %all-to-all-done.2 = bf16[128,64,128]{0,2,1:T(8,128)(2,1)S(1)} async-done(((bf16[128,64,128]{0,2,1:T(8,128)(2,1)}), bf16[128,64,128]{0,2,1:T(8,128)(2,1)S(1)}, u32[]{:S(2)}, u32[]{:S(2)}) %all-to-all-start.2) | async-done | bytes 2097184 | tf_op jit(solution)/shard_map/all_to_all | solution.py:73
  48.0 6.3 all-to-all-start.3
  54.4 4.1 copy.131
  59.5 22.4 %all-to-all-done.3 = bf16[128,64,128]{0,2,1:T(8,128)(2,1)S(1)} async-done(((bf16[128,64,128]{0,2,1:T(8,128)(2,1)}), bf16[128,64,128]{0,2,1:T(8,128)(2,1)S(1)}, u32[]{:S(2)}, u32[]{:S(2)}) %all-to-all-start.3) | async-done | bytes 2097184 | tf_op jit(solution)/shard_map/all_to_all | solution.py:74
  81.9 2.9 copy.138
  88.0 6.3 all-to-all-start
  94.3 12.8 %all-to-all-done = bf16[128,16,128]{2,0,1:T(8,128)(2,1)S(1)} async-done(((bf16[128,16,128]{2,0,1:T(8,128)(2,1)}), bf16[128,16,128]{2,0,1:T(8,128)(2,1)S(1)}, u32[]{:S(2)}, u32[]{:S(2)}) %all-to-all-start) | async-done | bytes 524320 | tf_op jit(solution)/shard_map/all_to_all | solution.py:75
  108.1 4.2 all-to-all-start.1
  112.4 62.5 %all-reduce.5.cloned.1.call-done = bf16[2,512,4,128]{3,1,2,0:T(8,128)(2,1)} async-done(((bf16[2,512,4,128]{3,1,2,0:T(8,128)(2,1)}), bf16[2,512,4,128]{3,1,2,0:T(8,128)(2,1)}) %all-reduce.5.cloned.1.call-update) | async-done | bytes 1048592 | tf_op jit(solution)/shard_map/psum | solution.py:23
  177.0 17.3 %while.80 = (s32[]{:T(128)}, f32[4,512]{1,0:T(4,128)S(1)}, f32[4,512]{1,0:T(4,128)}, f32[4,512,128]{2,1,0:T(8,128)S(1)}, bf16[4,512,128]{2,1,0:T(8,128)(2,1)S(1)...) while((s32[]{:T(128)}, f32[4,512]{1,0:T(4,128)S(1)}, ...), condition=%wide.region_11.12_spmd.clone, body=%wide.region_8.11_spmd.clone.sunk | while | flops 550505472 | bytes 14049409 | solution.py:147
  196.6 3.1 collective-permute-start
  203.5 3.1 copy.132
  206.6 2.5 broadcast.160.clone
  209.1 41.4 %while.77 = (s32[]{:T(128)}, f32[4,512,4]{1,2,0:T(4,128)S(1)}, f32[4,512,4]{1,2,0:T(4,128)S(1)}, f32[4,512,4,128]{1,3,2,0:T(8,128)}, s32[4]{0:T(128)S(1)}, /*ind...) while((s32[]{:T(128)}, f32[4,512,4]{1,2,0:T(4,128)S(1)}, ...), condition=%wide.region_6.7_spmd, body=%wide.region_3.6_spmd.sunk | while | flops 1102573568 | bytes 29462812 | solution.py:122
  215.2 4.3 fusion.178
  225.6 4.3 fusion.178
  235.9 4.3 fusion.178
  246.3 4.3 fusion.178
  250.6 5.5 copy.134
  256.0 5.4 copy.135
  261.4 3.9 copy.143
  266.0 30.2 %all-gather.3 = f32[8,4,512]{2,1,0:T(4,128)S(1)} all-gather(f32[1,4,512]{2,1,0:T(4,128)S(1)} %bitcast.429), channel_id=2, replica_groups=mesh['head'=16,'blk'=8] {'blk'}, dimensions={0}, use_global_device_ids=true | all-gather | bytes 73728 | tf_op jit(solution)/shard_map/all_gather | solution.py:27
  296.2 28.2 %all-gather.4 = f32[8,4,512]{2,1,0:T(4,128)S(1)} all-gather(f32[1,4,512]{2,1,0:T(4,128)S(1)} %bitcast.428), channel_id=3, replica_groups=mesh['head'=16,'blk'=8] {'blk'}, dimensions={0}, use_global_device_ids=true | all-gather | bytes 73728 | tf_op jit(solution)/shard_map/all_gather | solution.py:27
  325.7 15.1 %while.78 = (s32[]{:T(128)}, f32[4,512]{1,0:T(4,128)S(1)}, f32[4,512]{1,0:T(4,128)S(1)}, f32[4,512,128]{2,1,0:T(8,128)S(1)}, f32[8,4,512]{2,1,0:T(4,128)S(1)}, /...) while((s32[]{:T(128)}, f32[4,512]{1,0:T(4,128)S(1)}, ...), condition=%wide.region_13.14_spmd, body=%wide.region_12.13_spmd.sunk | while | flops 798725 | bytes 3227791 | solution.py:32
  327.9 2.1 fusion.180
  343.0 2.6 pad_maximum_fusion
  345.7 2.4 multiply_reduce_fusion
  348.2 32.9 %psum.22 = f32[2,4,512]{2,1,0:T(4,128)S(1)} all-reduce(f32[2,4,512]{2,1,0:T(4,128)S(1)} %maximum_select_fusion.1), channel_id=1, replica_groups=mesh['head'=16,'blk'=8] {'blk'}, use_global_device_ids=true, to_apply=%region_17.18 | all-reduce | flops 4096 | bytes 32768 | tf_op jit(solution)/shard_map/psum | solution.py:23
  381.6 4.6 copy.140
  386.3 30.8 %all-to-all-start.4 = ((bf16[2048,4,128]{2,1,0:T(4,128)(2,1)}), bf16[2048,4,128]{2,1,0:T(4,128)(2,1)}, u32[]{:S(2)}, u32[]{:S(2)}) async-start(bf16[2048,4,128]{2,1,0:T(4,128)(2,1)} %copy.140), calls=%async_computation.4 | async-start | bytes 4194304 | tf_op jit(solution)/shard_map/all_to_all | solution.py:164
  419.4 2.5 broadcast.160
  421.9 59.2 %while.79 = (s32[]{:T(128)}, f32[2560,128]{1,0:T(8,128)}, f32[2560,128]{1,0:T(8,128)}, f32[4,512,4,128]{1,3,2,0:T(8,128)}, s32[4]{0:T(128)S(1)}, /*index=5*/s32[...) while((s32[]{:T(128)}, f32[2560,128]{1,0:T(8,128)}, ...), condition=%wide.region_16.17_spmd, body=%wide.region_15.16_spmd.sunk | while | flops 2711748608 | bytes 74805720 | solution.py:210
  426.2 2.8 fusion.194
  429.0 4.6 fusion.192
  441.0 2.8 fusion.194
  443.8 4.6 fusion.192
  455.8 2.8 fusion.194
  458.6 4.6 fusion.192
  470.6 2.8 fusion.194
  473.4 4.6 fusion.192
  485.4 34.3 %while.81 = (s32[]{:T(128)}, f32[4,512,128]{2,1,0:T(8,128)S(1)}, f32[4,2048,128]{2,1,0:T(8,128)}, f32[4,2048,128]{2,1,0:T(8,128)}, bf16[4,512,128]{2,1,0:T(8,128...) while((s32[]{:T(128)}, f32[4,512,128]{2,1,0:T(8,128)S(1)}, ...), condition=%wide.region_19.20_spmd.clone, body=%wide.region_18.19_spmd.clone.sunk | while | flops 1349849088 | bytes 27543752 | solution.py:241
  491.3 2.7 fusion.213
  499.9 2.7 fusion.213
  508.4 2.6 fusion.213
  517.0 2.7 fusion.213
  520.6 3.5 reduce_sum.79
  524.1 3.6 reduce_sum.78
  529.5 2.9 pad_maximum_fusion.2
  532.4 5.7 all-to-all-start.6
  538.8 4.5 copy.146
  543.3 5.3 copy.147
  548.7 2.7 slice.213
  551.4 76.1 %all-reduce.7.cloned.1.call-done = f32[4,512,128]{2,1,0:T(8,128)} async-done(((f32[4,512,128]{2,1,0:T(8,128)}), f32[4,512,128]{2,1,0:T(8,128)}) %all-reduce.7.cloned.1.call-update) | async-done | bytes 1048592 | tf_op jit(solution)/shard_map/psum | solution.py:244
  630.4 10.7 %copy.148 = bf16[2048,4,128]{2,1,0:T(4,128)(2,1)} copy(bf16[2048,4,128]{2,0,1:T(8,128)(2,1)S(1)} %pad_maximum_fusion.1) | data formatting | bytes 4194304 | tf_op jit(solution)/shard_map/concatenate | solution.py:246
  641.1 10.5 %all-to-all-start.5 = ((bf16[2048,4,128]{2,1,0:T(4,128)(2,1)}), bf16[2048,4,128]{2,1,0:T(4,128)(2,1)}, u32[]{:S(2)}, u32[]{:S(2)}) async-start(bf16[2048,4,128]{2,1,0:T(4,128)(2,1)} %copy.148), calls=%async_computation.5 | async-start | bytes 4194304 | tf_op jit(solution)/shard_map/all_to_all | solution.py:276
  651.6 3.2 copy.141
  654.8 4.0 copy.142
  658.8 4.1 copy.155
  667.0 12.4 %all-to-all-done.5 = bf16[2048,4,128]{2,1,0:T(4,128)(2,1)} async-done(((bf16[2048,4,128]{2,1,0:T(4,128)(2,1)}), bf16[2048,4,128]{2,1,0:T(4,128)(2,1)}, u32[]{:S(2)}, u32[]{:S(2)}) %all-to-all-start.5) | async-done | bytes 2097184 | tf_op jit(solution)/shard_map/all_to_all | solution.py:276
  681.2 2.6 copy.150
  683.8 4.1 copy.156
  (327 shorter events, 140.3 us)
Async XLA Ops:
  7.2 79.9 %copy-start = (bf16[128,1024]{1,0:T(8,128)(2,1)S(1)}, bf16[128,1024]{1,0:T(8,128)(2,1)}, u32[]{:S(2)}) copy-start(bf16[128,1024]{1,0:T(8,128)(2,1)} %param.16) | copy-start | bytes 786436
  11.3 35.4 %all-to-all-start.2 = ((bf16[128,64,128]{0,2,1:T(8,128)(2,1)}), bf16[128,64,128]{0,2,1:T(8,128)(2,1)S(1)}, u32[]{:S(2)}, u32[]{:S(2)}) async-start(bf16[128,64,128]{0,2,1:T(8,128)(2,1)} %bitcast.404), calls=%async_computation.2 | async-start | bytes 4194304 | tf_op jit(solution)/shard_map/all_to_all | solution.py:73
  46.7 1.3 copy-start.12
  48.0 33.9 %all-to-all-start.3 = ((bf16[128,64,128]{0,2,1:T(8,128)(2,1)}), bf16[128,64,128]{0,2,1:T(8,128)(2,1)S(1)}, u32[]{:S(2)}, u32[]{:S(2)}) async-start(bf16[128,64,128]{0,2,1:T(8,128)(2,1)} %bitcast.403), calls=%async_computation.3 | async-start | bytes 4194304 | tf_op jit(solution)/shard_map/all_to_all | solution.py:74
  54.3 120.5 %all-reduce.5.cloned.1.call-start = ((), (), s32[]{:S(2)}) async-start(), calls=%async_computation.7 | async-start | bytes 2097152 | tf_op jit(solution)/shard_map/psum | solution.py:23
  81.9 5.1 copy-start.11
  84.8 9.5 %copy-start.23 = (bf16[128,1024]{1,0:T(8,128)(2,1)S(1)}, bf16[128,1024]{1,0:T(8,128)(2,1)}, u32[]{:S(2)}) copy-start(bf16[128,1024]{1,0:T(8,128)(2,1)} %param.17) | copy-start | bytes 786436
  88.0 19.1 %all-to-all-start = ((bf16[128,16,128]{2,0,1:T(8,128)(2,1)}), bf16[128,16,128]{2,0,1:T(8,128)(2,1)S(1)}, u32[]{:S(2)}, u32[]{:S(2)}) async-start(bf16[128,16,128]{2,0,1:T(8,128)(2,1)} %bitcast.26), calls=%async_computation | async-start | bytes 1048576 | tf_op jit(solution)/shard_map/all_to_all | solution.py:75
  108.1 68.9 %all-to-all-start.1 = ((bf16[128,16,128]{2,0,1:T(8,128)(2,1)}), bf16[128,16,128]{2,0,1:T(8,128)(2,1)S(1)}, u32[]{:S(2)}, u32[]{:S(2)}) async-start(bf16[128,16,128]{2,0,1:T(8,128)(2,1)} %bitcast.30), calls=%async_computation.1 | async-start | bytes 1048576 | tf_op jit(solution)/shard_map/all_to_all | solution.py:76
  112.3 212.1 %all-gather.7.cloned.1.call-start = ((), (), s32[]{:S(2)}) async-start(), calls=%async_computation.9 | async-start | bytes 9437184 | tf_op jit(solution)/shard_map/all_gather | solution.py:27
  177.0 18.4 %copy-start.33 = (s32[62]{0:T(128)S(1)}, s32[62]{0:T(128)}, u32[]{:S(2)}) copy-start(s32[62]{0:T(128)} %param.19) | copy-start | bytes 748
  194.4 1.0 copy-start.31
  194.4 9.0 %copy-start.6 = (bf16[2048,128]{1,0:T(8,128)(2,1)}, bf16[2048,128]{1,0:T(8,128)(2,1)S(1)}, u32[]{:S(2)}) copy-start(bf16[2048,128]{1,0:T(8,128)(2,1)S(1)} %get-tuple-element.1282) | copy-start | bytes 1572868
  194.4 9.0 %copy-start.14 = (bf16[4,512,128]{2,1,0:T(8,128)(2,1)}, bf16[4,512,128]{2,1,0:T(8,128)(2,1)S(1)}, u32[]{:S(2)}) copy-start(bf16[4,512,128]{2,1,0:T(8,128)(2,1)S(1)} %get-tuple-element.1296) | copy-start | bytes 1572868
  194.4 12.1 %copy-start.2 = (bf16[2048,128]{1,0:T(8,128)(2,1)}, bf16[2048,128]{1,0:T(8,128)(2,1)S(1)}, u32[]{:S(2)}) copy-start(bf16[2048,128]{1,0:T(8,128)(2,1)S(1)} %get-tuple-element.1278) | copy-start | bytes 1572868
  196.6 5.9 collective-permute-start
  203.4 5.7 copy-start.24
  203.4 5.7 copy-start.26
  203.4 5.7 copy-start.27
  203.4 5.7 copy-start.28
  203.5 5.7 copy-start.29
  250.6 5.5 copy-start.4
  265.3 30.9 %copy-start.30 = (f32[4,512]{1,0:T(4,128)S(1)}, f32[4,512]{1,0:T(4,128)}, u32[]{:S(2)}) copy-start(f32[4,512]{1,0:T(4,128)} %get-tuple-element.431) | copy-start | bytes 24580
  340.8 2.2 slice-start
  343.0 2.6 copy-start.13
  386.3 146.1 %all-to-all-start.4 = ((bf16[2048,4,128]{2,1,0:T(4,128)(2,1)}), bf16[2048,4,128]{2,1,0:T(4,128)(2,1)}, u32[]{:S(2)}, u32[]{:S(2)}) async-start(bf16[2048,4,128]{2,1,0:T(4,128)(2,1)} %copy.140), calls=%async_computation.4 | async-start | bytes 4194304 | tf_op jit(solution)/shard_map/all_to_all | solution.py:164
  417.1 4.9 copy-start.5
  421.9 63.4 %copy-start.3 = (bf16[2048,128]{1,0:T(8,128)(2,1)S(1)}, bf16[2048,128]{1,0:T(8,128)(2,1)}, u32[]{:S(2)}) copy-start(bf16[2048,128]{1,0:T(8,128)(2,1)} %copy-done.2) | copy-start | bytes 1572868
  424.2 1.3 copy-start.16
  424.2 2.0 copy-start.22
  429.0 4.7 copy-start.17
  429.0 4.7 copy-start.8
  435.0 1.8 copy-start.9
  439.0 1.3 copy-start.16
  439.0 2.0 copy-start.22
  443.8 4.7 copy-start.17
  443.8 4.7 copy-start.8
  449.8 1.7 copy-start.9
  453.8 1.3 copy-start.16
  453.8 2.0 copy-start.22
  458.6 4.7 copy-start.17
  458.6 4.7 copy-start.8
  464.6 1.8 copy-start.9
  468.6 1.3 copy-start.16
  468.6 2.0 copy-start.22
  473.4 4.7 copy-start.17
  473.4 4.7 copy-start.8
  479.4 1.8 copy-start.9
  484.0 43.8 %collective-permute-start.1 = (f32[2,512,128]{2,1,0:T(8,128)}, f32[2,512,128]{2,1,0:T(8,128)S(1)}, u32[]{:S(2)}, u32[]{:S(2)}) collective-permute-start(f32[2,512,128]{2,1,0:T(8,128)} %pad_maximum_fusion.5), channel_id=1, source_target_pairs={{1,0},{2,1},{3,2},{4,3},{5,4},{6,5},{7,6},{9,8},{10,9},{11,10},{12... | collective-permute-start | bytes 1572872 | tf_op jit(solution)/shard_map/ppermute | solution.py:18
  485.4 2.7 copy-start.7
  485.4 2.7 copy-start.15
  494.0 2.7 copy-start.7
  494.0 2.7 copy-start.15
  502.5 2.7 copy-start.7
  502.5 2.7 copy-start.15
  511.1 2.7 copy-start.7
  511.1 2.7 copy-start.15
  524.1 3.7 copy-start.18
  524.1 5.1 copy-start.10
  527.8 1.5 copy-start.21
  532.4 108.7 %all-to-all-start.6 = ((f32[2048,2,128]{2,1,0:T(2,128)}), f32[2048,2,128]{2,1,0:T(2,128)S(1)}, u32[]{:S(2)}, u32[]{:S(2)}) async-start(f32[2048,2,128]{2,1,0:T(2,128)} %pad_maximum_fusion.2), calls=%async_computation.6 | async-start | bytes 4194304 | tf_op jit(solution)/shard_map/all_to_all | solution.py:264
  538.1 89.4 %all-reduce.7.cloned.1.call-start = ((), (), s32[]{:S(2)}) async-start(), calls=%async_computation.8 | async-start | bytes 2097152 | tf_op jit(solution)/shard_map/psum | solution.py:244
  641.1 38.2 %all-to-all-start.5 = ((bf16[2048,4,128]{2,1,0:T(4,128)(2,1)}), bf16[2048,4,128]{2,1,0:T(4,128)(2,1)}, u32[]{:S(2)}, u32[]{:S(2)}) async-start(bf16[2048,4,128]{2,1,0:T(4,128)(2,1)} %copy.148), calls=%async_computation.5 | async-start | bytes 4194304 | tf_op jit(solution)/shard_map/all_to_all | solution.py:276
  681.2 6.7 copy-start.1
  (4 other events, 3.5 us)
Sparse Core Ops, SparseCore 0:
  87.2 87.6 all-reduce.4
  195.5 111.5 all-gather.6
  541.4 86.0 all-reduce.6
where the time goes:
time: 703 us; the launch traced here: 695 us
  waiting for transfers between devices  212 us (30%)
  local copies, waits for them, and re-layouts  124 us (18%)
  matrix products  108 us (15%)
  blocking collectives  91.2 us (13%)
  starting transfers between devices  76.3 us (11%)
  other arithmetic  62.5 us (9%)
  between operations  14.5 us (2%)
    psum x1, waiting for transfers between devices, shards(): question_total = lax.psum(quest_query_parts, 'blk')  76.1 us
    psum x1, waiting for transfers between devices, broadcast(): return lax.psum(block, axis)  62.5 us
    all_gather x2, blocking collectives, merged_2(): gathered = jax.tree.map(lambda a: lax.all_gather(a, axis), part)  58.3 us
    psum x1, blocking collectives, broadcast(): return lax.psum(block, axis)  32.9 us
    all_to_all x1, starting transfers between devices, shards(): lax.all_to_all(attended_head, 'head', split_axis=0, concat_axis=1, tiled=...  30.8 us
    all_to_all x1, waiting for transfers between devices, shards(): lax.all_to_all(query_matrix, 'head', split_axis=1, concat_axis=0, tiled=T...  23.5 us
    all_to_all x1, waiting for transfers between devices, shards(): lax.all_to_all(output_adjoint, 'head', split_axis=1, concat_axis=0, tiled...  22.4 us
    unnamed x60, local copies, waits for them, and re-layouts  22.1 us
  transfers between devices with their start and end apart: 12, of which 7 were waited for; matrix products, arithmetic and copies ran while one was open for 32% of the time, Pallas kernels for 0%

commit v1 on v0

--- a/solution.py
+++ b/solution.py
@@ -241,7 +241,7 @@
     quest_query_parts, quest_key_parts, quest_value_parts = lax.map(
         question_backward, (question_query, question_grad, shared_stat[0], shared_stat[1])
     )
-    question_total = lax.psum(quest_query_parts, "blk")
+    question_total = jnp.sum(lax.all_gather(quest_query_parts, "blk"), axis=0)
     question_added = jnp.where(holder, jnp.moveaxis(question_total, 0, 1), 0.0)
     query_grads = jnp.concatenate(
         [query_grads[:question_start], query_grads[question_start:] + question_added]

time: 703 us -> 650 us (0.925)
  waiting for transfers between devices: 212 us -> 166 us
    psum x1 -> x0, waiting for transfers between devices: 76.1 us -> none  [shards(): question_total = lax.psum(quest_query_parts, 'blk')]
    all_to_all x1, waiting for transfers between devices: 0.01 us -> 31 us  [shards(): lax.all_to_all(attended_head, 'head', split_axis=0, concat_axis=1, tiled=...]
    unnamed x60 -> x64, local copies, waits for them, and re-layouts: 22.1 us -> 21.1 us
  transfers between devices with their start and end apart: 12 -> 12, of which waited for: 7 -> 7; matrix products, arithmetic and copies ran while one was open for 32% -> 31% of each run, Pallas kernels for 0% -> 0%
where the time goes in v1:
time: 650 us; the launch traced here: 642 us
  waiting for transfers between devices  166 us (26%)
  local copies, waits for them, and re-layouts  120 us (18%)
  matrix products  104 us (16%)
  blocking collectives  91.5 us (14%)
  starting transfers between devices  71.8 us (11%)
  other arithmetic  67.2 us (10%)
  between operations  14.6 us (2%)
    psum x1, waiting for transfers between devices, broadcast(): return lax.psum(block, axis)  62.5 us
    all_gather x2, blocking collectives, merged_2(): gathered = jax.tree.map(lambda a: lax.all_gather(a, axis), part)  58.4 us
    psum x1, blocking collectives, broadcast(): return lax.psum(block, axis)  33.2 us
    all_to_all x1, starting transfers between devices, shards(): lax.all_to_all(attended_head, 'head', split_axis=0, concat_axis=1, tiled=...  31.2 us
    all_to_all x1, waiting for transfers between devices, shards(): lax.all_to_all(attended_head, 'head', split_axis=0, concat_axis=1, tiled=...  31 us
    all_to_all x1, waiting for transfers between devices, shards(): lax.all_to_all(query_matrix, 'head', split_axis=1, concat_axis=0, tiled=T...  23.5 us
    all_to_all x1, waiting for transfers between devices, shards(): lax.all_to_all(output_adjoint, 'head', split_axis=1, concat_axis=0, tiled...  22.4 us
    unnamed x64, local copies, waits for them, and re-layouts  21.1 us
  transfers between devices with their start and end apart: 12, of which 7 were waited for; matrix products, arithmetic and copies ran while one was open for 31% of the time, Pallas kernels for 0%

profile of v1, /device:TPU:1, one launch (start us, length us, event | category | flops | bytes accessed | tf_op | source)
XLA Modules:
  0.0 641.9 jit_solution(14386879455046194820)
XLA Ops:
  7.2 4.1 copy.130
  11.3 7.8 %all-to-all-start.2 = ((bf16[128,64,128]{0,2,1:T(8,128)(2,1)}), bf16[128,64,128]{0,2,1:T(8,128)(2,1)S(1)}, u32[]{:S(2)}, u32[]{:S(2)}) async-start(bf16[128,64,128]{0,2,1:T(8,128)(2,1)} %bitcast.406), calls=%async_computation.2 | async-start | bytes 4194304 | tf_op jit(solution)/shard_map/all_to_all | solution.py:73
  19.1 4.1 copy.137
  23.2 23.5 %all-to-all-done.2 = bf16[128,64,128]{0,2,1:T(8,128)(2,1)S(1)} async-done(((bf16[128,64,128]{0,2,1:T(8,128)(2,1)}), bf16[128,64,128]{0,2,1:T(8,128)(2,1)S(1)}, u32[]{:S(2)}, u32[]{:S(2)}) %all-to-all-start.2) | async-done | bytes 2097184 | tf_op jit(solution)/shard_map/all_to_all | solution.py:73
  48.0 6.3 all-to-all-start.3
  54.4 4.1 copy.131
  59.5 22.4 %all-to-all-done.3 = bf16[128,64,128]{0,2,1:T(8,128)(2,1)S(1)} async-done(((bf16[128,64,128]{0,2,1:T(8,128)(2,1)}), bf16[128,64,128]{0,2,1:T(8,128)(2,1)S(1)}, u32[]{:S(2)}, u32[]{:S(2)}) %all-to-all-start.3) | async-done | bytes 2097184 | tf_op jit(solution)/shard_map/all_to_all | solution.py:74
  81.9 2.9 copy.138
  88.0 6.3 all-to-all-start
  94.3 12.8 %all-to-all-done = bf16[128,16,128]{2,0,1:T(8,128)(2,1)S(1)} async-done(((bf16[128,16,128]{2,0,1:T(8,128)(2,1)}), bf16[128,16,128]{2,0,1:T(8,128)(2,1)S(1)}, u32[]{:S(2)}, u32[]{:S(2)}) %all-to-all-start) | async-done | bytes 524320 | tf_op jit(solution)/shard_map/all_to_all | solution.py:75
  108.1 4.2 all-to-all-start.1
  112.4 62.5 %all-reduce.4.cloned.1.call-done = bf16[2,512,4,128]{3,1,2,0:T(8,128)(2,1)} async-done(((bf16[2,512,4,128]{3,1,2,0:T(8,128)(2,1)}), bf16[2,512,4,128]{3,1,2,0:T(8,128)(2,1)}) %all-reduce.4.cloned.1.call-update) | async-done | bytes 1048592 | tf_op jit(solution)/shard_map/psum | solution.py:23
  177.1 17.3 %while.80 = (s32[]{:T(128)}, f32[4,512]{1,0:T(4,128)S(1)}, f32[4,512]{1,0:T(4,128)}, f32[4,512,128]{2,1,0:T(8,128)S(1)}, bf16[4,512,128]{2,1,0:T(8,128)(2,1)S(1)...) while((s32[]{:T(128)}, f32[4,512]{1,0:T(4,128)S(1)}, ...), condition=%wide.region_11.12_spmd.clone, body=%wide.region_8.11_spmd.clone.sunk | while | flops 550505472 | bytes 14049409 | solution.py:147
  196.7 3.1 collective-permute-start
  203.5 3.1 copy.132
  206.6 2.5 broadcast.160.clone
  209.2 41.4 %while.77 = (s32[]{:T(128)}, f32[4,512,4]{1,2,0:T(4,128)S(1)}, f32[4,512,4]{1,2,0:T(4,128)S(1)}, f32[4,512,4,128]{1,3,2,0:T(8,128)}, s32[4]{0:T(128)S(1)}, /*ind...) while((s32[]{:T(128)}, f32[4,512,4]{1,2,0:T(4,128)S(1)}, ...), condition=%wide.region_6.7_spmd, body=%wide.region_3.6_spmd.sunk | while | flops 1102573568 | bytes 29462812 | solution.py:122
  215.3 4.3 fusion.178
  225.6 4.3 fusion.178
  236.0 4.3 fusion.178
  246.3 4.3 fusion.178
  250.6 6.0 copy.134
  256.6 5.4 copy.135
  262.0 3.9 copy.143
  266.6 30.3 %all-gather.4 = f32[8,4,512]{2,1,0:T(4,128)S(1)} all-gather(f32[1,4,512]{2,1,0:T(4,128)S(1)} %bitcast.431), channel_id=2, replica_groups=mesh['head'=16,'blk'=8] {'blk'}, dimensions={0}, use_global_device_ids=true | all-gather | bytes 73728 | tf_op jit(solution)/shard_map/all_gather | solution.py:27
  296.9 28.1 %all-gather.5 = f32[8,4,512]{2,1,0:T(4,128)S(1)} all-gather(f32[1,4,512]{2,1,0:T(4,128)S(1)} %bitcast.430), channel_id=3, replica_groups=mesh['head'=16,'blk'=8] {'blk'}, dimensions={0}, use_global_device_ids=true | all-gather | bytes 73728 | tf_op jit(solution)/shard_map/all_gather | solution.py:27
  326.3 15.1 %while.78 = (s32[]{:T(128)}, f32[4,512]{1,0:T(4,128)S(1)}, f32[4,512]{1,0:T(4,128)S(1)}, f32[4,512,128]{2,1,0:T(8,128)S(1)}, f32[8,4,512]{2,1,0:T(4,128)S(1)}, /...) while((s32[]{:T(128)}, f32[4,512]{1,0:T(4,128)S(1)}, ...), condition=%wide.region_13.14_spmd, body=%wide.region_12.13_spmd.sunk | while | flops 798725 | bytes 3227791 | solution.py:32
  326.3 2.1 fusion.180
  332.8 2.1 fusion.180
  335.0 2.1 fusion.180
  337.2 2.1 fusion.180
  344.2 2.7 pad_maximum_fusion
  346.9 2.5 multiply_reduce_fusion
  349.4 33.2 %psum.15 = f32[2,4,512]{2,1,0:T(4,128)S(1)} all-reduce(f32[2,4,512]{2,1,0:T(4,128)S(1)} %maximum_select_fusion.1), channel_id=1, replica_groups=mesh['head'=16,'blk'=8] {'blk'}, use_global_device_ids=true, to_apply=%region_17.18 | all-reduce | flops 4096 | bytes 32768 | tf_op jit(solution)/shard_map/psum | solution.py:23
  383.6 26.6 %while.81 = (s32[]{:T(128)}, f32[4,512,128]{2,1,0:T(8,128)}, f32[4,2048,128]{2,1,0:T(8,128)}, f32[4,2048,128]{2,1,0:T(8,128)}, bf16[4,512,128]{2,1,0:T(8,128)(2,...) while((s32[]{:T(128)}, f32[4,512,128]{2,1,0:T(8,128)}, ...), condition=%wide.region_19.20_spmd.clone, body=%wide.region_18.19_spmd.clone.sunk | while | flops 1349849088 | bytes 23349392 | solution.py:241
  412.5 2.5 broadcast.160
  415.0 59.6 %while.79 = (s32[]{:T(128)}, f32[2560,128]{1,0:T(8,128)}, f32[2560,128]{1,0:T(8,128)}, f32[4,512,4,128]{1,3,2,0:T(8,128)}, s32[4]{0:T(128)S(1)}, /*index=5*/s32[...) while((s32[]{:T(128)}, f32[2560,128]{1,0:T(8,128)}, ...), condition=%wide.region_16.17_spmd, body=%wide.region_15.16_spmd.sunk | while | flops 2711748608 | bytes 74805720 | solution.py:210
  419.4 2.8 fusion.194
  422.2 4.6 fusion.192
  434.3 2.8 fusion.194
  437.1 4.6 fusion.192
  449.2 2.8 fusion.194
  452.0 4.6 fusion.192
  464.1 2.8 fusion.194
  466.9 4.6 fusion.192
  479.0 4.7 copy.140
  483.7 31.2 %all-to-all-start.4 = ((bf16[2048,4,128]{2,1,0:T(4,128)(2,1)}), bf16[2048,4,128]{2,1,0:T(4,128)(2,1)}, u32[]{:S(2)}, u32[]{:S(2)}) async-start(bf16[2048,4,128]{2,1,0:T(4,128)(2,1)} %copy.140), calls=%async_computation.4 | async-start | bytes 4194304 | tf_op jit(solution)/shard_map/all_to_all | solution.py:164
  514.9 3.5 reduce_sum.89
  518.4 3.7 reduce_sum.88
  523.8 2.9 pad_maximum_fusion.2
  526.7 31.0 %all-to-all-done.4 = bf16[2048,4,128]{2,1,0:T(4,128)(2,1)} async-done(((bf16[2048,4,128]{2,1,0:T(4,128)(2,1)}), bf16[2048,4,128]{2,1,0:T(4,128)(2,1)}, u32[]{:S(2)}, u32[]{:S(2)}) %all-to-all-start.4) | async-done | bytes 2097184 | tf_op jit(solution)/shard_map/all_to_all | solution.py:164
  557.7 5.2 all-to-all-start.6
  562.9 4.5 copy.146
  567.5 5.3 copy.147
  572.7 2.6 slice.213
  575.4 3.9 reduce_sum.87
  582.2 10.7 %copy.148 = bf16[2048,4,128]{2,1,0:T(4,128)(2,1)} copy(bf16[2048,4,128]{2,0,1:T(8,128)(2,1)S(1)} %pad_maximum_fusion.1) | data formatting | bytes 4194304 | tf_op jit(solution)/shard_map/concatenate | solution.py:246
  592.9 6.1 all-to-all-start.5
  599.0 3.2 copy.141
  602.2 4.0 copy.142
  606.2 4.1 copy.155
  614.4 12.1 %all-to-all-done.5 = bf16[2048,4,128]{2,1,0:T(4,128)(2,1)} async-done(((bf16[2048,4,128]{2,1,0:T(4,128)(2,1)}), bf16[2048,4,128]{2,1,0:T(4,128)(2,1)}, u32[]{:S(2)}, u32[]{:S(2)}) %all-to-all-start.5) | async-done | bytes 2097184 | tf_op jit(solution)/shard_map/all_to_all | solution.py:276
  628.4 2.6 copy.150
  631.0 4.1 copy.156
  (316 shorter events, 136.5 us)
Async XLA Ops:
  7.2 79.9 %copy-start = (bf16[128,1024]{1,0:T(8,128)(2,1)S(1)}, bf16[128,1024]{1,0:T(8,128)(2,1)}, u32[]{:S(2)}) copy-start(bf16[128,1024]{1,0:T(8,128)(2,1)} %param.16) | copy-start | bytes 786436
  11.3 35.4 %all-to-all-start.2 = ((bf16[128,64,128]{0,2,1:T(8,128)(2,1)}), bf16[128,64,128]{0,2,1:T(8,128)(2,1)S(1)}, u32[]{:S(2)}, u32[]{:S(2)}) async-start(bf16[128,64,128]{0,2,1:T(8,128)(2,1)} %bitcast.406), calls=%async_computation.2 | async-start | bytes 4194304 | tf_op jit(solution)/shard_map/all_to_all | solution.py:73
  46.7 1.3 copy-start.10
  48.0 33.9 %all-to-all-start.3 = ((bf16[128,64,128]{0,2,1:T(8,128)(2,1)}), bf16[128,64,128]{0,2,1:T(8,128)(2,1)S(1)}, u32[]{:S(2)}, u32[]{:S(2)}) async-start(bf16[128,64,128]{0,2,1:T(8,128)(2,1)} %bitcast.405), calls=%async_computation.3 | async-start | bytes 4194304 | tf_op jit(solution)/shard_map/all_to_all | solution.py:74
  54.3 120.6 %all-reduce.4.cloned.1.call-start = ((), (), s32[]{:S(2)}) async-start(), calls=%async_computation.7 | async-start | bytes 2097152 | tf_op jit(solution)/shard_map/psum | solution.py:23
  81.9 5.1 copy-start.9
  84.8 9.5 %copy-start.21 = (bf16[128,1024]{1,0:T(8,128)(2,1)S(1)}, bf16[128,1024]{1,0:T(8,128)(2,1)}, u32[]{:S(2)}) copy-start(bf16[128,1024]{1,0:T(8,128)(2,1)} %param.17) | copy-start | bytes 786436
  88.0 19.1 %all-to-all-start = ((bf16[128,16,128]{2,0,1:T(8,128)(2,1)}), bf16[128,16,128]{2,0,1:T(8,128)(2,1)S(1)}, u32[]{:S(2)}, u32[]{:S(2)}) async-start(bf16[128,16,128]{2,0,1:T(8,128)(2,1)} %bitcast.26), calls=%async_computation | async-start | bytes 1048576 | tf_op jit(solution)/shard_map/all_to_all | solution.py:75
  108.1 68.9 %all-to-all-start.1 = ((bf16[128,16,128]{2,0,1:T(8,128)(2,1)}), bf16[128,16,128]{2,0,1:T(8,128)(2,1)S(1)}, u32[]{:S(2)}, u32[]{:S(2)}) async-start(bf16[128,16,128]{2,0,1:T(8,128)(2,1)} %bitcast.30), calls=%async_computation.1 | async-start | bytes 1048576 | tf_op jit(solution)/shard_map/all_to_all | solution.py:76
  112.3 212.7 %all-gather.9.cloned.1.call-start = ((), (), s32[]{:S(2)}) async-start(), calls=%async_computation.8 | async-start | bytes 9437184 | tf_op jit(solution)/shard_map/all_gather | solution.py:27
  177.1 18.4 %copy-start.33 = (s32[62]{0:T(128)S(1)}, s32[62]{0:T(128)}, u32[]{:S(2)}) copy-start(s32[62]{0:T(128)} %param.19) | copy-start | bytes 748
  194.4 1.0 copy-start.18
  194.4 1.0 copy-start.31
  194.4 8.1 %copy-start.12 = (bf16[4,512,128]{2,1,0:T(8,128)(2,1)}, bf16[4,512,128]{2,1,0:T(8,128)(2,1)S(1)}, u32[]{:S(2)}) copy-start(bf16[4,512,128]{2,1,0:T(8,128)(2,1)S(1)} %get-tuple-element.1295) | copy-start | bytes 1572868
  194.5 9.0 %copy-start.4 = (bf16[2048,128]{1,0:T(8,128)(2,1)}, bf16[2048,128]{1,0:T(8,128)(2,1)S(1)}, u32[]{:S(2)}) copy-start(bf16[2048,128]{1,0:T(8,128)(2,1)S(1)} %get-tuple-element.1282) | copy-start | bytes 1572868
  195.4 379.9 %all-gather.11.cloned.1.call-start = ((), (), s32[]{:S(2)}) async-start(), calls=%async_computation.9 | async-start | bytes 9437184 | tf_op jit(solution)/shard_map/all_gather | solution.py:244
  195.8 0.8 copy-start.23
  196.7 5.9 collective-permute-start
  203.5 5.7 copy-start.22
  203.5 5.7 copy-start.24
  203.5 5.7 copy-start.25
  203.5 5.7 copy-start.26
  203.5 5.7 copy-start.28
  250.6 6.0 copy-start.2
  250.6 15.3 %copy-start.29 = (f32[4,512,4]{1,2,0:T(4,128)}, f32[4,512,4]{1,2,0:T(4,128)S(1)}, u32[]{:S(2)}) copy-start(f32[4,512,4]{1,2,0:T(4,128)S(1)} %get-tuple-element.429) | copy-start | bytes 98308
  250.6 15.3 %copy-start.27 = (f32[4,512,4]{1,2,0:T(4,128)}, f32[4,512,4]{1,2,0:T(4,128)S(1)}, u32[]{:S(2)}) copy-start(f32[4,512,4]{1,2,0:T(4,128)S(1)} %get-tuple-element.435) | copy-start | bytes 98308
  265.9 0.7 copy-start.32
  265.9 31.0 %copy-start.30 = (f32[4,512]{1,0:T(4,128)S(1)}, f32[4,512]{1,0:T(4,128)}, u32[]{:S(2)}) copy-start(f32[4,512]{1,0:T(4,128)} %get-tuple-element.431) | copy-start | bytes 24580
  341.5 2.8 slice-start
  344.2 2.7 copy-start.11
  346.9 36.7 %copy-start.5 = (bf16[2048,128]{1,0:T(8,128)(2,1)S(1)}, bf16[2048,128]{1,0:T(8,128)(2,1)}, u32[]{:S(2)}) copy-start(bf16[2048,128]{1,0:T(8,128)(2,1)} %copy-done.4) | copy-start | bytes 1572868
  346.9 36.7 %copy-start.13 = (bf16[4,512,128]{2,1,0:T(8,128)(2,1)S(1)}, bf16[4,512,128]{2,1,0:T(8,128)(2,1)}, u32[]{:S(2)}) copy-start(bf16[4,512,128]{2,1,0:T(8,128)(2,1)} %copy-done.12) | copy-start | bytes 1572868
  346.9 36.7 %copy-start.14 = (bf16[4,512,128]{2,1,0:T(8,128)(2,1)S(1)}, bf16[4,512,128]{2,1,0:T(8,128)(2,1)}, u32[]{:S(2)}) copy-start(bf16[4,512,128]{2,1,0:T(8,128)(2,1)} %get-tuple-element.1245) | copy-start | bytes 1572868
  410.2 4.8 copy-start.3
  417.4 1.3 copy-start.15
  417.4 2.0 copy-start.20
  422.2 4.7 copy-start.16
  422.2 4.7 copy-start.6
  428.2 1.8 copy-start.7
  432.3 1.3 copy-start.15
  432.3 2.0 copy-start.20
  437.1 4.7 copy-start.16
  437.1 4.7 copy-start.6
  443.1 1.7 copy-start.7
  447.2 1.3 copy-start.15
  447.2 2.0 copy-start.20
  452.0 4.7 copy-start.16
  452.0 4.7 copy-start.6
  457.9 1.8 copy-start.7
  462.1 1.3 copy-start.15
  462.1 2.0 copy-start.20
  466.9 4.7 copy-start.16
  466.9 4.7 copy-start.6
  472.9 1.7 copy-start.7
  477.6 44.5 %collective-permute-start.1 = (f32[2,512,128]{2,1,0:T(8,128)}, f32[2,512,128]{2,1,0:T(8,128)S(1)}, u32[]{:S(2)}, u32[]{:S(2)}) collective-permute-start(f32[2,512,128]{2,1,0:T(8,128)} %pad_maximum_fusion.5), channel_id=1, source_target_pairs={{1,0},{2,1},{3,2},{4,3},{5,4},{6,5},{7,6},{9,8},{10,9},{11,10},{12... | collective-permute-start | bytes 1572872 | tf_op jit(solution)/shard_map/ppermute | solution.py:18
  483.7 74.0 %all-to-all-start.4 = ((bf16[2048,4,128]{2,1,0:T(4,128)(2,1)}), bf16[2048,4,128]{2,1,0:T(4,128)(2,1)}, u32[]{:S(2)}, u32[]{:S(2)}) async-start(bf16[2048,4,128]{2,1,0:T(4,128)(2,1)} %copy.140), calls=%async_computation.4 | async-start | bytes 4194304 | tf_op jit(solution)/shard_map/all_to_all | solution.py:164
  518.4 3.8 copy-start.17
  518.4 5.2 copy-start.8
  522.1 1.5 copy-start.19
  557.7 35.2 %all-to-all-start.6 = ((f32[2048,2,128]{2,1,0:T(2,128)}), f32[2048,2,128]{2,1,0:T(2,128)S(1)}, u32[]{:S(2)}, u32[]{:S(2)}) async-start(f32[2048,2,128]{2,1,0:T(2,128)} %pad_maximum_fusion.2), calls=%async_computation.6 | async-start | bytes 4194304 | tf_op jit(solution)/shard_map/all_to_all | solution.py:264
  592.9 33.6 %all-to-all-start.5 = ((bf16[2048,4,128]{2,1,0:T(4,128)(2,1)}), bf16[2048,4,128]{2,1,0:T(4,128)(2,1)}, u32[]{:S(2)}, u32[]{:S(2)}) async-start(bf16[2048,4,128]{2,1,0:T(4,128)(2,1)} %copy.148), calls=%async_computation.5 | async-start | bytes 4194304 | tf_op jit(solution)/shard_map/all_to_all | solution.py:276
  628.4 6.7 %copy-start.1 = (bf16[128,1024]{1,0:T(8,128)(2,1)S(1)}, bf16[128,1024]{1,0:T(8,128)(2,1)}, u32[]{:S(2)}) copy-start(bf16[128,1024]{1,0:T(8,128)(2,1)} %param.16) | copy-start | bytes 786436
Sparse Core Ops, SparseCore 0:
  87.2 87.6 all-reduce.3
  195.6 111.5 all-gather.8
  410.4 152.6 all-gather.10
